TPU v7x, 1024 devices: a whole 4x8x16 slice. The times are simulated.
1024 devices in a mesh: blk: 32 (over x, y_lo, core), group: 32 (over z, y_hi).
Axes of the slice: x: 4, y: 8 (y_hi: 2, y_lo: 4; y = y_hi * 4 + y_lo), z: 16, core: 2. Of those that a mesh axis runs over, the one named last changes fastest.
Arguments:
- row_factors: float32 [524288, 256], P(('blk', 'group')), may hold values from -0.45 to 0.45
- col_factors: float32 [524288, 256], P(('blk', 'group')), may hold values from -0.45 to 0.45
- tile_values: bfloat16 [5, 8192, 128, 128], P(None, ('blk', 'group')), may hold values from -4 to 4
- tile_coords: int32 [5, 8192, 2], P(None, ('blk', 'group')), may hold values from 0 to 3, as said below
- tile_counts: int32 [5, 1024], P(None, ('blk', 'group')), may hold values from 2 to 8, as said below
Outputs:
- rows_out: float32 [524288, 256], P(('blk', 'group'))
- cols_out: float32 [524288, 256], P(('blk', 'group'))
Inputs may be any that keep to these rules, and one draw needn't show every extreme that they name: `tile_coords`: the 8 entries of one device and stratum name distinct tiles; the row tile is below 4, the column tile below 4. `tile_counts`: in every stratum some device lists 8 live tiles.
All inputs are finite; a program needn't handle non-finite values.
Results may differ from a plain program's by a relative error of at most 0.005.
Values sent between devices are 32-bit elements; how exact they have to be, the bound alone decides.
A program may use at most 32 MiB of HBM per device.

v0:
```python
import jax
import jax.numpy as jnp
from jax import lax
from jax.sharding import PartitionSpec as P

STRATA = 5


LEARN_RATE = 0.03
DECAY_RATE = 0.1


def shifted(block, axis, distance):
    devices = range(lax.axis_size(axis))
    route = [((i - distance) % len(devices), i) for i in devices]
    return lax.ppermute(block, axis, route)


def picker(positions, extent, live_mask):
    return (positions[:, None] == jnp.arange(extent)[None, :]).astype(jnp.float32) * live_mask[
        :, None
    ]


def padded_parts(row_block, col_block, values, tile_pos, live_mask):
    tile = values.shape[1]
    rank = row_block.shape[1]
    row_pick = picker(tile_pos[:, 0], row_block.shape[0] // tile, live_mask)
    col_pick = picker(tile_pos[:, 1], col_block.shape[0] // tile, live_mask)
    row_half = row_block.astype(jnp.bfloat16).reshape(-1, tile, rank)
    col_half = col_block.astype(jnp.bfloat16).reshape(-1, tile, rank)
    row_sel = jnp.einsum(
        "tk,kia->tia", row_pick.astype(jnp.bfloat16), row_half, preferred_element_type=jnp.float32
    ).astype(jnp.bfloat16)
    col_sel = jnp.einsum(
        "tk,kja->tja", col_pick.astype(jnp.bfloat16), col_half, preferred_element_type=jnp.float32
    ).astype(jnp.bfloat16)
    estimate = jnp.einsum("tia,tja->tij", row_sel, col_sel, preferred_element_type=jnp.float32)
    residue = (values.astype(jnp.float32) - estimate).astype(jnp.bfloat16)
    return (residue, row_sel, col_sel, row_pick, col_pick)


def padded_rows(parts):
    residue, row_sel, col_sel, row_pick, col_pick = parts
    terms = jnp.einsum("tij,tja->tia", residue, col_sel, preferred_element_type=jnp.float32)
    summed = jnp.einsum("tk,tia->kia", row_pick, terms, precision=lax.Precision.HIGHEST)
    return summed.reshape(-1, summed.shape[2])


def padded_cols(parts):
    residue, row_sel, col_sel, row_pick, col_pick = parts
    terms = jnp.einsum("tij,tia->tja", residue, row_sel, preferred_element_type=jnp.float32)
    summed = jnp.einsum("tk,tja->kja", col_pick, terms, precision=lax.Precision.HIGHEST)
    return summed.reshape(-1, summed.shape[2])


def rotate(col_block, stratum):
    if stratum == 2:
        return shifted(col_block, "group", 1)
    return shifted(col_block, "blk", 1)


def per_device(row_factors, col_factors, tile_values, tile_coords, tile_counts):
    row_block = row_factors
    col_block = col_factors
    for stratum in range(STRATA):
        values = tile_values[stratum]
        tile_pos = tile_coords[stratum]
        tile_count = tile_counts[stratum, 0]
        live_mask = (jnp.arange(values.shape[0]) < tile_count).astype(jnp.float32)
        parts = padded_parts(row_block, col_block, values, tile_pos, live_mask)
        grad_rows = padded_rows(parts)
        grad_cols = padded_cols(parts)
        row_block = row_block + LEARN_RATE * (grad_rows - DECAY_RATE * row_block)
        col_block = col_block + LEARN_RATE * (grad_cols - DECAY_RATE * col_block)
        if stratum + 1 < STRATA:
            col_block = rotate(col_block, stratum)
    return (row_block, col_block)


def solution(mesh):
    return jax.shard_map(
        per_device,
        mesh=mesh,
        in_specs=(
            P(("blk", "group"), None),
            P(("blk", "group"), None),
            P(None, ("blk", "group"), None, None),
            P(None, ("blk", "group"), None),
            P(None, ("blk", "group")),
        ),
        out_specs=(P(("blk", "group"), None), P(("blk", "group"), None)),
        check_vma=False,
    )
```

profile of v0, /device:TPU:6, one launch (start us, length us, event | category | flops | bytes accessed | tf_op | source)
XLA Modules:
  0.0 103.8 jit_solution(2239440648864601405)
XLA Ops:
  0.6 1.5 %fusion.190 = (s32[1,1]{0,1:T(1,128)}, s32[1,1]{0,1:T(1,128)}, s32[1,1]{0,1:T(1,128)}, s32[1,1]{0,1:T(1,128)}, s32[1,1]{0,1:T(1,128)}) fusion(s32[5,1]{0,1:T(1,128)} %param.9), kind=kLoop, calls=%fused_computation.254 | loop fusion | bytes 40 | tf_op jit(solution)/shard_map/slice | solution.py:69
  2.1 0.6 compare_convert_fusion.4
  2.7 0.8 slice_bitcast_fusion
  3.4 1.1 %convert_element_type.187 = bf16[512,256]{1,0:T(8,128)(2,1)S(1)} convert(f32[512,256]{1,0:T(8,128)} %param.6) | non-fusion elementwise | flops 131072 | bytes 786432 | tf_op jit(solution)/shard_map/convert_element_type | solution.py:31
  4.5 1.2 %convert_element_type.184 = bf16[512,256]{1,0:T(8,128)(2,1)S(1)} convert(f32[512,256]{1,0:T(8,128)} %param.5) | non-fusion elementwise | flops 131072 | bytes 786432 | tf_op jit(solution)/shard_map/convert_element_type | solution.py:30
  5.7 0.4 convolution_convert_fusion.8
  6.0 0.4 convolution_convert_fusion.9
  6.4 0.3 fusion
  6.7 0.3 fusion.72
  7.1 1.5 %fusion.21 = f32[4,128,256]{2,0,1:T(4,128)S(1)} fusion(f32[8,128,256]{2,1,0:T(8,128)S(1)} %fusion.72, s32[8]{0:T(128)S(1)} %get-tuple-element.18, f32[8]{0:T(128)S(1)} %compare_convert_fusion.4), kind=kOutput, calls=%fused_computation.36 | convolution fusion | flops 12582976 | bytes 1572928 | tf_op jit(solution)/shard_map/tk,tja->kja/dot_general | solution.py:53
  8.6 0.1 copy.29
  8.8 1.9 %collective-permute-start = (f32[512,256]{1,0:T(8,128)S(1)}, f32[512,256]{1,0:T(8,128)S(1)}, u32[]{:S(2)}, u32[]{:S(2)}) collective-permute-start(f32[512,256]{1,0:T(8,128)S(1)} %fusion.42), channel_id=1, source_target_pairs={{992,0},{0,32},{32,64},{64,96},{96,128},{128,160},{160,192},{192,2... | collective-permute-start | bytes 1572872 | tf_op jit(solution)/shard_map/ppermute | solution.py:16
  10.7 0.3 fusion.69
  11.0 0.7 compare_convert_fusion
  11.7 0.7 compare_convert_fusion.2
  12.3 0.6 compare_convert_fusion.3
  13.0 1.5 %fusion.23 = f32[4,128,256]{2,0,1:T(4,128)S(1)} fusion(f32[8,128,256]{2,1,0:T(8,128)S(1)} %fusion.69, f32[8]{0:T(128)S(1)} %compare_convert_fusion.4, s32[8]{0:T(128)S(1)} %get-tuple-element.17), kind=kOutput, calls=%fused_computation.38 | convolution fusion | flops 12582976 | bytes 1572928 | tf_op jit(solution)/shard_map/tk,tia->kia/dot_general | solution.py:46
  14.5 0.6 compare_convert_fusion.1
  15.2 0.1 copy.27
  15.4 0.4 convolution_convert_fusion.7
  15.7 6.3 %collective-permute-done = f32[512,256]{1,0:T(8,128)S(1)} collective-permute-done((f32[512,256]{1,0:T(8,128)S(1)}, f32[512,256]{1,0:T(8,128)S(1)}, u32[]{:S(2)}, u32[]{:S(2)}) %collective-permute-start) | collective-permute-done | bytes 524320 | tf_op jit(solution)/shard_map/ppermute | solution.py:16
  22.0 0.4 convolution_convert_fusion.6
  22.4 0.3 fusion.1
  22.7 0.3 fusion.66
  23.1 0.3 fusion.63
  23.4 1.5 %fusion.17 = f32[4,128,256]{2,0,1:T(4,128)S(1)} fusion(f32[8,128,256]{2,1,0:T(8,128)S(1)} %fusion.66, s32[8]{0:T(128)S(1)} %get-tuple-element.26, f32[8]{0:T(128)S(1)} %compare_convert_fusion.3), kind=kOutput, calls=%fused_computation.32 | convolution fusion | flops 12582976 | bytes 1572928 | tf_op jit(solution)/shard_map/tk,tja->kja/dot_general | solution.py:53
  24.9 0.1 copy.35
  25.0 1.5 %fusion.19 = f32[4,128,256]{2,0,1:T(4,128)S(1)} fusion(f32[8,128,256]{2,1,0:T(8,128)S(1)} %fusion.63, f32[8]{0:T(128)S(1)} %compare_convert_fusion.3, s32[8]{0:T(128)S(1)} %get-tuple-element.27), kind=kOutput, calls=%fused_computation.34 | convolution fusion | flops 12582976 | bytes 1572928 | tf_op jit(solution)/shard_map/tk,tia->kia/dot_general | solution.py:46
  26.4 0.1 copy.33
  26.7 2.1 %collective-permute-start.1 = (f32[512,256]{1,0:T(8,128)S(1)}, f32[512,256]{1,0:T(8,128)S(1)}, u32[]{:S(2)}, u32[]{:S(2)}) collective-permute-start(f32[512,256]{1,0:T(8,128)S(1)} %fusion.38), channel_id=1, source_target_pairs={{992,0},{0,32},{32,64},{64,96},{96,128},{128,160},{160,192},{192,2... | collective-permute-start | bytes 1572872 | tf_op jit(solution)/shard_map/ppermute | solution.py:16
  28.8 0.2 fusion.188
  28.9 0.4 convolution_convert_fusion.5
  29.3 10.6 %collective-permute-done.1 = f32[512,256]{1,0:T(8,128)S(1)} collective-permute-done((f32[512,256]{1,0:T(8,128)S(1)}, f32[512,256]{1,0:T(8,128)S(1)}, u32[]{:S(2)}, u32[]{:S(2)}) %collective-permute-start.1) | collective-permute-done | bytes 524320 | tf_op jit(solution)/shard_map/ppermute | solution.py:16
  39.9 0.4 convolution_convert_fusion.4
  40.2 0.3 fusion.2
  40.6 0.3 fusion.60
  40.9 0.3 fusion.57
  41.2 1.5 %fusion.13 = f32[4,128,256]{2,0,1:T(4,128)S(1)} fusion(f32[8,128,256]{2,1,0:T(8,128)S(1)} %fusion.60, s32[8]{0:T(128)S(1)} %get-tuple-element.14, f32[8]{0:T(128)S(1)} %compare_convert_fusion.2), kind=kOutput, calls=%fused_computation.28 | convolution fusion | flops 12582976 | bytes 1572928 | tf_op jit(solution)/shard_map/tk,tja->kja/dot_general | solution.py:53
  42.7 0.1 copy.41
  42.9 7.7 %collective-permute-start.2 = (f32[512,256]{1,0:T(8,128)S(1)}, f32[512,256]{1,0:T(8,128)S(1)}, u32[]{:S(2)}, u32[]{:S(2)}) collective-permute-start(f32[512,256]{1,0:T(8,128)S(1)} %fusion.34), channel_id=1, source_target_pairs={{31,0},{0,1},{1,2},{2,3},{3,4},{4,5},{5,6},{6,7},{7,8},{8,9},{9,10... | collective-permute-start | bytes 1572872 | tf_op jit(solution)/shard_map/ppermute | solution.py:16
  50.7 1.5 %fusion.15 = f32[4,128,256]{2,0,1:T(4,128)S(1)} fusion(f32[8,128,256]{2,1,0:T(8,128)S(1)} %fusion.57, f32[8]{0:T(128)S(1)} %compare_convert_fusion.2, s32[8]{0:T(128)S(1)} %get-tuple-element.13), kind=kOutput, calls=%fused_computation.30 | convolution fusion | flops 12582976 | bytes 1572928 | tf_op jit(solution)/shard_map/tk,tia->kia/dot_general | solution.py:46
  52.3 0.4 convolution_convert_fusion.3
  52.7 28.4 %collective-permute-done.2 = f32[512,256]{1,0:T(8,128)S(1)} collective-permute-done((f32[512,256]{1,0:T(8,128)S(1)}, f32[512,256]{1,0:T(8,128)S(1)}, u32[]{:S(2)}, u32[]{:S(2)}) %collective-permute-start.2) | collective-permute-done | bytes 524320 | tf_op jit(solution)/shard_map/ppermute | solution.py:16
  81.2 0.4 convolution_convert_fusion.2
  81.5 0.3 fusion.3
  81.9 0.3 fusion.54
  82.2 0.3 fusion.51
  82.5 1.5 %fusion.9 = f32[4,128,256]{2,0,1:T(4,128)S(1)} fusion(f32[8,128,256]{2,1,0:T(8,128)S(1)} %fusion.54, s32[8]{0:T(128)S(1)} %get-tuple-element.24, f32[8]{0:T(128)S(1)} %compare_convert_fusion.1), kind=kOutput, calls=%fused_computation.24 | convolution fusion | flops 12582976 | bytes 1572928 | tf_op jit(solution)/shard_map/tk,tja->kja/dot_general | solution.py:53
  84.0 0.1 copy.47
  84.2 2.1 %collective-permute-start.3 = (f32[512,256]{1,0:T(8,128)S(1)}, f32[512,256]{1,0:T(8,128)S(1)}, u32[]{:S(2)}, u32[]{:S(2)}) collective-permute-start(f32[512,256]{1,0:T(8,128)S(1)} %fusion.30), channel_id=1, source_target_pairs={{992,0},{0,32},{32,64},{64,96},{96,128},{128,160},{160,192},{192,2... | collective-permute-start | bytes 1572872 | tf_op jit(solution)/shard_map/ppermute | solution.py:16
  86.3 1.5 %fusion.11 = f32[4,128,256]{2,0,1:T(4,128)S(1)} fusion(f32[8,128,256]{2,1,0:T(8,128)S(1)} %fusion.51, f32[8]{0:T(128)S(1)} %compare_convert_fusion.1, s32[8]{0:T(128)S(1)} %get-tuple-element.25), kind=kOutput, calls=%fused_computation.26 | convolution fusion | flops 12582976 | bytes 1572928 | tf_op jit(solution)/shard_map/tk,tia->kia/dot_general | solution.py:46
  87.8 0.1 copy.45
  87.9 0.2 fusion.187
  88.1 0.4 convolution_convert_fusion.1
  88.5 8.9 %collective-permute-done.3 = f32[512,256]{1,0:T(8,128)S(1)} collective-permute-done((f32[512,256]{1,0:T(8,128)S(1)}, f32[512,256]{1,0:T(8,128)S(1)}, u32[]{:S(2)}, u32[]{:S(2)}) %collective-permute-start.3) | collective-permute-done | bytes 524320 | tf_op jit(solution)/shard_map/ppermute | solution.py:16
  97.4 0.4 convolution_convert_fusion
  97.8 0.3 fusion.4
  98.1 0.3 fusion.48
  98.5 0.3 fusion.45
  98.8 1.5 %fusion.5 = f32[4,128,256]{2,0,1:T(4,128)S(1)} fusion(f32[8,128,256]{2,1,0:T(8,128)S(1)} %fusion.48, s32[8]{0:T(128)S(1)} %get-tuple-element.10, f32[8]{0:T(128)S(1)} %compare_convert_fusion), kind=kOutput, calls=%fused_computation.20 | convolution fusion | flops 12582976 | bytes 1572928 | tf_op jit(solution)/shard_map/tk,tja->kja/dot_general | solution.py:53
  100.2 0.1 copy.52
  100.3 1.5 %fusion.7 = f32[4,128,256]{2,0,1:T(4,128)S(1)} fusion(f32[8,128,256]{2,1,0:T(8,128)S(1)} %fusion.45, f32[8]{0:T(128)S(1)} %compare_convert_fusion, s32[8]{0:T(128)S(1)} %get-tuple-element.9), kind=kOutput, calls=%fused_computation.22 | convolution fusion | flops 12582976 | bytes 1572928 | tf_op jit(solution)/shard_map/tk,tia->kia/dot_general | solution.py:46
  101.9 1.0 fusion.28
  102.9 0.9 fusion.26
  (21 shorter events, 0.9 us)
Async XLA Ops:
  4.5 1.9 %copy-start.2 = (bf16[5,8,128,128]{3,2,1,0:T(8,128)(2,1)S(1)}, bf16[5,8,128,128]{3,2,1,0:T(8,128)(2,1)}, u32[]{:S(2)}) copy-start(bf16[5,8,128,128]{3,2,1,0:T(8,128)(2,1)} %param.7) | copy-start | bytes 3932164
  7.1 1.6 %copy-start.1 = (f32[512,256]{1,0:T(8,128)S(1)}, f32[512,256]{1,0:T(8,128)}, u32[]{:S(2)}) copy-start(f32[512,256]{1,0:T(8,128)} %param.6) | copy-start | bytes 1572868
  8.8 13.2 %collective-permute-start = (f32[512,256]{1,0:T(8,128)S(1)}, f32[512,256]{1,0:T(8,128)S(1)}, u32[]{:S(2)}, u32[]{:S(2)}) collective-permute-start(f32[512,256]{1,0:T(8,128)S(1)} %fusion.42), channel_id=1, source_target_pairs={{992,0},{0,32},{32,64},{64,96},{96,128},{128,160},{160,192},{192,2... | collective-permute-start | bytes 1572872 | tf_op jit(solution)/shard_map/ppermute | solution.py:16
  13.0 2.3 %copy-start = (f32[512,256]{1,0:T(8,128)S(1)}, f32[512,256]{1,0:T(8,128)}, u32[]{:S(2)}) copy-start(f32[512,256]{1,0:T(8,128)} %param.5) | copy-start | bytes 1572868
  26.7 13.2 %collective-permute-start.1 = (f32[512,256]{1,0:T(8,128)S(1)}, f32[512,256]{1,0:T(8,128)S(1)}, u32[]{:S(2)}, u32[]{:S(2)}) collective-permute-start(f32[512,256]{1,0:T(8,128)S(1)} %fusion.38), channel_id=1, source_target_pairs={{992,0},{0,32},{32,64},{64,96},{96,128},{128,160},{160,192},{192,2... | collective-permute-start | bytes 1572872 | tf_op jit(solution)/shard_map/ppermute | solution.py:16
  42.9 38.2 %collective-permute-start.2 = (f32[512,256]{1,0:T(8,128)S(1)}, f32[512,256]{1,0:T(8,128)S(1)}, u32[]{:S(2)}, u32[]{:S(2)}) collective-permute-start(f32[512,256]{1,0:T(8,128)S(1)} %fusion.34), channel_id=1, source_target_pairs={{31,0},{0,1},{1,2},{2,3},{3,4},{4,5},{5,6},{6,7},{7,8},{8,9},{9,10... | collective-permute-start | bytes 1572872 | tf_op jit(solution)/shard_map/ppermute | solution.py:16
  84.2 13.2 %collective-permute-start.3 = (f32[512,256]{1,0:T(8,128)S(1)}, f32[512,256]{1,0:T(8,128)S(1)}, u32[]{:S(2)}, u32[]{:S(2)}) collective-permute-start(f32[512,256]{1,0:T(8,128)S(1)} %fusion.30), channel_id=1, source_target_pairs={{992,0},{0,32},{32,64},{64,96},{96,128},{128,160},{160,192},{192,2... | collective-permute-start | bytes 1572872 | tf_op jit(solution)/shard_map/ppermute | solution.py:16
where the time goes:
time: 104 us
  waiting for transfers between devices  54.2 us (52%)
  matrix products  23.1 us (22%)
  starting transfers between devices  13.9 us (13%)
  other arithmetic  8.21 us (8%)
  local copies, waits for them, and re-layouts  3.29 us (3%)
  between operations  1.16 us (1%)
    ppermute x4, waiting for transfers between devices, shifted(): return lax.ppermute(block, axis, route)  54.2 us
    ppermute x4, starting transfers between devices, shifted(): return lax.ppermute(block, axis, route)  13.9 us
    dot_general x5, matrix products, padded_rows(): jnp.einsum('tk,tia->kia', row_pick, terms, precision=lax.Precision.HIGHEST)  7.39 us
    dot_general x5, matrix products, padded_cols(): jnp.einsum('tk,tja->kja', col_pick, terms, precision=lax.Precision.HIGHEST)  7.39 us
    convert_element_type x5, other arithmetic, per_device(): live_mask = (jnp.arange(values.shape[0]) < tile_count).astype(jnp.float32)  3.13 us
  transfers between devices with their start and end apart: 4, of which 4 were waited for; matrix products, arithmetic and copies ran while one was open for 9% of the time, Pallas kernels for 0%

commit v1 on v0

v1 whole, which is shorter than its diff:
```python
import functools

import jax
import jax.numpy as jnp
from jax import lax
from jax.experimental import pallas as pl
from jax.experimental.pallas import tpu as pltpu
from jax.sharding import PartitionSpec as P

STRATA = 5
TILE = 128
MOST = 8
PIECES = 4

LEARN_RATE = 0.03
DECAY_RATE = 0.1

MESH = pl.DeviceIdType.MESH


def shift_axis(stratum):
    return "group" if stratum == 2 else "blk"


def neighbour(axis, distance, size):
    return {axis: lax.rem(lax.axis_index(axis) + size + distance, size)}


def find_slots(counts, coords, slots, lives, stratum, row_tiles, col_tiles):
    places = []
    for k in range(MOST):
        place = coords[stratum, 0, k] * col_tiles + coords[stratum, 1, k]
        places.append(jnp.where(k < counts[stratum], place, -1))
    for place in range(row_tiles * col_tiles):
        slot = jnp.int32(0)
        live = jnp.int32(0)
        for k in range(MOST):
            hit = places[k] == place
            slot = jnp.where(hit, k, slot)
            live = jnp.where(hit, 1, live)
        slots[stratum, place] = slot
        lives[stratum, place] = live.astype(jnp.float32)


def kernel(
    sizes, counts, coords, rows_in, cols_in, tiles_in, rows_out, cols_out,
    u, a, gu, held, sent, slots, lives, load_sem, send_sem, recv_sem, *tiles,
):
    rows = rows_in.shape[0]
    cols = cols_in.shape[0]
    row_tiles, col_tiles = rows // TILE, cols // TILE
    piece = cols // PIECES

    loads = [
        pltpu.make_async_copy(rows_in, u, load_sem.at[0]),
        pltpu.make_async_copy(cols_in, held.at[0], load_sem.at[1]),
    ]
    for stratum in range(STRATA):
        loads.append(pltpu.make_async_copy(tiles_in.at[stratum], tiles[stratum], load_sem.at[2 + stratum]))
    for load in loads:
        load.start()

    barrier = pltpu.get_barrier_semaphore()
    for axis in ("blk", "group"):
        pl.semaphore_signal(barrier, inc=1, device_id=neighbour(axis, -1, sizes[axis]), device_id_type=MESH)

    for stratum in range(STRATA):
        find_slots(counts, coords, slots, lives, stratum, row_tiles, col_tiles)

    copies = {}
    loads[0].wait()
    loads[1].wait()
    a[...] = u[...].astype(jnp.bfloat16)
    for stratum in range(STRATA):
        loads[2 + stratum].wait()
        last = stratum + 1 == STRATA
        for j in range(PIECES):
            span = pl.ds(j * piece, piece)
            if stratum:
                copies[stratum - 1, j].wait_recv()
            block = held[stratum, span, :]
            half = block.astype(jnp.bfloat16)
            estimate = lax.dot_general(
                a[...], half, (((1,), (1,)), ((), ())), preferred_element_type=jnp.float32
            )
            residues = []
            for i in range(row_tiles):
                place = i * col_tiles + j * piece // TILE
                values = tiles[stratum][slots[stratum, place]].astype(jnp.float32)
                error = values - estimate[i * TILE : (i + 1) * TILE, :]
                residues.append((error * lives[stratum, place]).astype(jnp.bfloat16))
            residue = jnp.concatenate(residues, axis=0)
            grad_cols = lax.dot_general(
                residue, a[...], (((0,), (0,)), ((), ())), preferred_element_type=jnp.float32
            )
            new_cols = block + LEARN_RATE * (grad_cols - DECAY_RATE * block)
            if last:
                cols_out[span, :] = new_cols
            else:
                sent[stratum, span, :] = new_cols
                if stratum == 0 and j == 0:
                    pl.semaphore_wait(barrier, 2)
                axis = shift_axis(stratum)
                copies[stratum, j] = pltpu.make_async_remote_copy(
                    src_ref=sent.at[stratum, span],
                    dst_ref=held.at[stratum + 1, span],
                    send_sem=send_sem.at[stratum, j],
                    recv_sem=recv_sem.at[stratum, j],
                    device_id=neighbour(axis, 1, sizes[axis]),
                    device_id_type=MESH,
                )
                copies[stratum, j].start()
            part = jnp.dot(residue, half, preferred_element_type=jnp.float32)
            if j == 0:
                gu[...] = part
            elif j + 1 < PIECES:
                gu[...] += part
            else:
                new_rows = u[...] + LEARN_RATE * ((gu[...] + part) - DECAY_RATE * u[...])
                if last:
                    rows_out[...] = new_rows
                else:
                    u[...] = new_rows
                    a[...] = new_rows.astype(jnp.bfloat16)
    for copy in copies.values():
        copy.wait_send()


def solution(mesh):
    sizes = dict(mesh.shape)

    def per_device(row_factors, col_factors, tile_values, tile_coords, tile_counts):
        rows, rank = row_factors.shape
        cols = col_factors.shape[0]
        out = pltpu.VMEM((rows, rank), jnp.float32)
        smem = pl.BlockSpec(memory_space=pltpu.SMEM)
        hbm = pl.BlockSpec(memory_space=pl.ANY)
        vmem = pl.BlockSpec(memory_space=pltpu.VMEM)
        places = (rows // TILE) * (cols // TILE)
        return pl.pallas_call(
            functools.partial(kernel, sizes),
            out_shape=(out, pltpu.VMEM((cols, rank), jnp.float32)),
            in_specs=[smem, smem, hbm, hbm, hbm],
            out_specs=(vmem, vmem),
            scratch_shapes=[
                pltpu.VMEM((rows, rank), jnp.float32),
                pltpu.VMEM((rows, rank), jnp.bfloat16),
                pltpu.VMEM((rows, rank), jnp.float32),
                pltpu.VMEM((STRATA, cols, rank), jnp.float32),
                pltpu.VMEM((STRATA - 1, cols, rank), jnp.float32),
                pltpu.SMEM((STRATA, places), jnp.int32),
                pltpu.SMEM((STRATA, places), jnp.float32),
                pltpu.SemaphoreType.DMA((2 + STRATA,)),
                pltpu.SemaphoreType.DMA((STRATA - 1, PIECES)),
                pltpu.SemaphoreType.DMA((STRATA - 1, PIECES)),
            ]
            + [pltpu.VMEM((MOST, TILE, TILE), jnp.bfloat16)] * STRATA,
            compiler_params=pltpu.CompilerParams(collective_id=0, has_side_effects=True),
            name="strata",
        )(
            tile_counts.reshape(STRATA),
            tile_coords.transpose(0, 2, 1),
            row_factors,
            col_factors,
            tile_values,
        )

    return jax.shard_map(
        per_device,
        mesh=mesh,
        in_specs=(
            P(("blk", "group"), None),
            P(("blk", "group"), None),
            P(None, ("blk", "group"), None, None),
            P(None, ("blk", "group"), None),
            P(None, ("blk", "group")),
        ),
        out_specs=(P(("blk", "group"), None), P(("blk", "group"), None)),
        check_vma=False,
    )
```

time: 104 us -> 74.8 us (0.72)
  the two profiles are of different devices: /device:TPU:6 before, /device:TPU:1 now
where the time goes in v1:
time: 74.8 us; the launch traced here: 74.6 us
  Pallas kernels  72.4 us (97%)
  local copies, waits for them, and re-layouts  1.59 us (2%)
    pallas_call x1, Pallas kernels, per_device(): pl.pallas_call(functools.partial(kernel, sizes), out_shape=(out, pltpu.VM...  72.4 us
    unnamed x2, local copies, waits for them, and re-layouts  1.59 us

profile of v1, /device:TPU:1, one launch (start us, length us, event | category | flops | bytes accessed | tf_op | source)
XLA Modules:
  0.0 74.6 jit_solution(2162920120061112042)
XLA Ops:
  0.6 72.4 %strata.1 = (f32[512,256]{1,0:T(8,128)S(1)}, f32[512,256]{1,0:T(8,128)S(1)}) custom-call(s32[5]{0:T(128)} %bitcast.3, s32[5,2,8]{2,1,0:T(2,128)} %bitcast.2, f32[512,256]{1,0:T(8,128)} %rows_in.1, f32[512,256]{1,0:T(8,128)} %cols_in.1, bf16[5,8,128,128]{3,2,1,0:T(8,128)(2,1)} %tiles_in.1), custom_call_target="tpu_custom_call" | custom-call | tf_op jit(solution)/shard_map/strata/pallas_call | solution.py:140
  73.0 0.8 %copy.9 = f32[512,256]{1,0:T(8,128)} copy(f32[512,256]{1,0:T(8,128)S(1)} %get-tuple-element.2) | data formatting | bytes 1048576
  73.8 0.8 %copy.10 = f32[512,256]{1,0:T(8,128)} copy(f32[512,256]{1,0:T(8,128)S(1)} %get-tuple-element.3) | data formatting | bytes 1048576

commit v2 on v1

--- a/solution.py
+++ b/solution.py
@@ -11,6 +11,7 @@
 TILE = 128
 MOST = 8
 PIECES = 4
+GATED = 2
 
 LEARN_RATE = 0.03
 DECAY_RATE = 0.1
@@ -44,7 +45,7 @@
 
 def kernel(
     sizes, counts, coords, rows_in, cols_in, tiles_in, rows_out, cols_out,
-    u, a, gu, held, sent, slots, lives, load_sem, send_sem, recv_sem, *tiles,
+    u, a, gu, held, sent, slots, lives, load_sem, send_sem, recv_sem, gate, *tiles,
 ):
     rows = rows_in.shape[0]
     cols = cols_in.shape[0]
@@ -61,17 +62,20 @@
         load.start()
 
     barrier = pltpu.get_barrier_semaphore()
-    for axis in ("blk", "group"):
-        pl.semaphore_signal(barrier, inc=1, device_id=neighbour(axis, -1, sizes[axis]), device_id_type=MESH)
+    for axis, distance in (("blk", -1), ("blk", 1), ("group", -1)):
+        pl.semaphore_signal(barrier, inc=1, device_id=neighbour(axis, distance, sizes[axis]), device_id_type=MESH)
 
-    for stratum in range(STRATA):
-        find_slots(counts, coords, slots, lives, stratum, row_tiles, col_tiles)
+    group = lax.axis_index("group")
+    gated = (group > 0) & (group + 1 < sizes["group"])
+    find_slots(counts, coords, slots, lives, 0, row_tiles, col_tiles)
 
     copies = {}
     loads[0].wait()
     loads[1].wait()
     a[...] = u[...].astype(jnp.bfloat16)
     for stratum in range(STRATA):
+        if stratum:
+            find_slots(counts, coords, slots, lives, stratum, row_tiles, col_tiles)
         loads[2 + stratum].wait()
         last = stratum + 1 == STRATA
         for j in range(PIECES):
@@ -99,7 +103,7 @@
             else:
                 sent[stratum, span, :] = new_cols
                 if stratum == 0 and j == 0:
-                    pl.semaphore_wait(barrier, 2)
+                    pl.semaphore_wait(barrier, 3)
                 axis = shift_axis(stratum)
                 copies[stratum, j] = pltpu.make_async_remote_copy(
                     src_ref=sent.at[stratum, span],
@@ -109,7 +113,21 @@
                     device_id=neighbour(axis, 1, sizes[axis]),
                     device_id_type=MESH,
                 )
-                copies[stratum, j].start()
+                if stratum != GATED:
+                    copies[stratum, j].start()
+                else:
+                    pl.when(jnp.logical_not(gated))(copies[stratum, j].start)
+                if stratum == GATED and j + 1 == PIECES:
+                    core = lax.rem(lax.axis_index("blk"), 2)
+                    mate = {"blk": lax.axis_index("blk") + 1 - 2 * core}
+
+                    @pl.when(gated)
+                    def _():
+                        pl.semaphore_signal(gate, inc=1, device_id=mate, device_id_type=MESH)
+                        pl.semaphore_wait(gate, 1)
+                        for at in range(PIECES):
+                            copies[stratum, at].start()
+
             part = jnp.dot(residue, half, preferred_element_type=jnp.float32)
             if j == 0:
                 gu[...] = part
@@ -153,6 +171,7 @@
                 pltpu.SemaphoreType.DMA((2 + STRATA,)),
                 pltpu.SemaphoreType.DMA((STRATA - 1, PIECES)),
                 pltpu.SemaphoreType.DMA((STRATA - 1, PIECES)),
+                pltpu.SemaphoreType.REGULAR,
             ]
             + [pltpu.VMEM((MOST, TILE, TILE), jnp.bfloat16)] * STRATA,
             compiler_params=pltpu.CompilerParams(collective_id=0, has_side_effects=True),

time: 74.8 us -> 60.6 us (0.81)
  the two profiles are of different devices: /device:TPU:1 before, /device:TPU:6 now
where the time goes in v2:
time: 60.6 us; the launch traced here: 60.1 us
  Pallas kernels  57.8 us (95%)
  local copies, waits for them, and re-layouts  1.59 us (3%)
  between operations  0.64 us (1%)
    pallas_call x1, Pallas kernels, per_device(): pl.pallas_call(functools.partial(kernel, sizes), out_shape=(out, pltpu.VM...  57.8 us
    unnamed x2, local copies, waits for them, and re-layouts  1.59 us

profile of v2, /device:TPU:6, one launch (start us, length us, event | category | flops | bytes accessed | tf_op | source)
XLA Modules:
  0.0 60.1 jit_solution(16048027740032756549)
XLA Ops:
  0.6 57.8 %strata.1 = (f32[512,256]{1,0:T(8,128)S(1)}, f32[512,256]{1,0:T(8,128)S(1)}) custom-call(s32[5]{0:T(128)} %bitcast.3, s32[5,2,8]{2,1,0:T(2,128)} %bitcast.2, f32[512,256]{1,0:T(8,128)} %rows_in.1, f32[512,256]{1,0:T(8,128)} %cols_in.1, bf16[5,8,128,128]{3,2,1,0:T(8,128)(2,1)} %tiles_in.1), custom_call_target="tpu_custom_call" | custom-call | tf_op jit(solution)/shard_map/strata/pallas_call | solution.py:158
  58.5 0.8 %copy.9 = f32[512,256]{1,0:T(8,128)} copy(f32[512,256]{1,0:T(8,128)S(1)} %get-tuple-element.2) | data formatting | bytes 1048576
  59.3 0.8 %copy.10 = f32[512,256]{1,0:T(8,128)} copy(f32[512,256]{1,0:T(8,128)S(1)} %get-tuple-element.3) | data formatting | bytes 1048576

commit v3 on v2

--- a/solution.py
+++ b/solution.py
@@ -44,21 +44,28 @@
 
 
 def kernel(
-    sizes, counts, coords, rows_in, cols_in, tiles_in, rows_out, cols_out,
-    u, a, gu, held, sent, slots, lives, load_sem, send_sem, recv_sem, gate, *tiles,
+    sizes, counts_in, coords_in, rows_in, cols_in, tiles_in, both_out,
+    u, a, gu, held, sent, slots, lives, load_sem, send_sem, recv_sem, gate, counts, coords, table_sem, *tiles,
 ):
     rows = rows_in.shape[0]
     cols = cols_in.shape[0]
+    rows_out, cols_out = both_out.at[pl.ds(0, rows)], both_out.at[pl.ds(rows, cols)]
     row_tiles, col_tiles = rows // TILE, cols // TILE
     piece = cols // PIECES
 
+    tables = [
+        pltpu.make_async_copy(counts_in, counts, table_sem.at[0]),
+        pltpu.make_async_copy(coords_in, coords, table_sem.at[1]),
+    ]
+    for table in tables:
+        table.start()
     loads = [
         pltpu.make_async_copy(rows_in, u, load_sem.at[0]),
         pltpu.make_async_copy(cols_in, held.at[0], load_sem.at[1]),
     ]
     for stratum in range(STRATA):
         loads.append(pltpu.make_async_copy(tiles_in.at[stratum], tiles[stratum], load_sem.at[2 + stratum]))
-    for load in loads:
+    for load in loads[:3]:
         load.start()
 
     barrier = pltpu.get_barrier_semaphore()
@@ -67,16 +74,21 @@
 
     group = lax.axis_index("group")
     gated = (group > 0) & (group + 1 < sizes["group"])
+    for table in tables:
+        table.wait()
     find_slots(counts, coords, slots, lives, 0, row_tiles, col_tiles)
 
     copies = {}
     loads[0].wait()
     loads[1].wait()
+    loads[2].wait()
+    for load in loads[3:]:
+        load.start()
     a[...] = u[...].astype(jnp.bfloat16)
     for stratum in range(STRATA):
         if stratum:
             find_slots(counts, coords, slots, lives, stratum, row_tiles, col_tiles)
-        loads[2 + stratum].wait()
+            loads[2 + stratum].wait()
         last = stratum + 1 == STRATA
         for j in range(PIECES):
             span = pl.ds(j * piece, piece)
@@ -150,16 +162,14 @@
     def per_device(row_factors, col_factors, tile_values, tile_coords, tile_counts):
         rows, rank = row_factors.shape
         cols = col_factors.shape[0]
-        out = pltpu.VMEM((rows, rank), jnp.float32)
-        smem = pl.BlockSpec(memory_space=pltpu.SMEM)
         hbm = pl.BlockSpec(memory_space=pl.ANY)
         vmem = pl.BlockSpec(memory_space=pltpu.VMEM)
         places = (rows // TILE) * (cols // TILE)
-        return pl.pallas_call(
+        both = pl.pallas_call(
             functools.partial(kernel, sizes),
-            out_shape=(out, pltpu.VMEM((cols, rank), jnp.float32)),
-            in_specs=[smem, smem, hbm, hbm, hbm],
-            out_specs=(vmem, vmem),
+            out_shape=pltpu.VMEM((rows + cols, rank), jnp.float32),
+            in_specs=[hbm, hbm, hbm, hbm, hbm],
+            out_specs=vmem,
             scratch_shapes=[
                 pltpu.VMEM((rows, rank), jnp.float32),
                 pltpu.VMEM((rows, rank), jnp.bfloat16),
@@ -172,6 +182,9 @@
                 pltpu.SemaphoreType.DMA((STRATA - 1, PIECES)),
                 pltpu.SemaphoreType.DMA((STRATA - 1, PIECES)),
                 pltpu.SemaphoreType.REGULAR,
+                pltpu.SMEM((STRATA,), jnp.int32),
+                pltpu.SMEM((STRATA, 2, MOST), jnp.int32),
+                pltpu.SemaphoreType.DMA((2,)),
             ]
             + [pltpu.VMEM((MOST, TILE, TILE), jnp.bfloat16)] * STRATA,
             compiler_params=pltpu.CompilerParams(collective_id=0, has_side_effects=True),
@@ -183,6 +196,7 @@
             col_factors,
             tile_values,
         )
+        return both[:rows], both[rows:]
 
     return jax.shard_map(
         per_device,

time: 60.6 us -> 59.3 us (0.979)
  Pallas kernels: 57.8 us -> 57.1 us
    unnamed x2 -> x0, local copies, waits for them, and re-layouts: 1.59 us -> none
    slice x0 -> x1, local copies, waits for them, and re-layouts: none -> 1.03 us  [per_device(): return (both[:rows], both[rows:])]
    pallas_call x1, Pallas kernels: 57.8 us -> 57.1 us  [per_device(): pl.pallas_call(functools.partial(kernel, sizes), out_shape=pltpu.VMEM((ro...]
where the time goes in v3:
time: 59.3 us; the launch traced here: 58.8 us
  Pallas kernels  57.1 us (96%)
  local copies, waits for them, and re-layouts  1.03 us (2%)
  between operations  0.64 us (1%)
    pallas_call x1, Pallas kernels, per_device(): pl.pallas_call(functools.partial(kernel, sizes), out_shape=pltpu.VMEM((ro...  57.1 us

profile of v3, /device:TPU:6, one launch (start us, length us, event | category | flops | bytes accessed | tf_op | source)
XLA Modules:
  0.0 58.8 jit_solution(6920742947747894092)
XLA Ops:
  0.6 57.1 %strata.1 = f32[1024,256]{1,0:T(8,128)S(1)} custom-call(s32[5]{0:T(128)} %bitcast.3, s32[5,2,8]{2,1,0:T(2,128)} %bitcast.2, f32[512,256]{1,0:T(8,128)} %rows_in.1, f32[512,256]{1,0:T(8,128)} %cols_in.1, bf16[5,8,128,128]{3,2,1,0:T(8,128)(2,1)} %tiles_in.1), custom_call_target="tpu_custom_call" | custom-call | tf_op jit(solution)/shard_map/strata/pallas_call | solution.py:168
  57.7 1.0 %fusion = (f32[512,256]{1,0:T(8,128)}, f32[512,256]{1,0:T(8,128)}) fusion(f32[1024,256]{1,0:T(8,128)S(1)} %strata.1), kind=kLoop, calls=%fused_computation | loop fusion | bytes 2097152 | tf_op jit(solution)/shard_map/slice | solution.py:199

commit v4 on v3

--- a/solution.py
+++ b/solution.py
@@ -86,13 +86,16 @@
         load.start()
     a[...] = u[...].astype(jnp.bfloat16)
     for stratum in range(STRATA):
+        if stratum == 1:
+            find_slots(counts, coords, slots, lives, stratum, row_tiles, col_tiles)
         if stratum:
-            find_slots(counts, coords, slots, lives, stratum, row_tiles, col_tiles)
             loads[2 + stratum].wait()
         last = stratum + 1 == STRATA
         for j in range(PIECES):
             span = pl.ds(j * piece, piece)
             if stratum:
+                if j + 1 == PIECES and not last:
+                    find_slots(counts, coords, slots, lives, stratum + 1, row_tiles, col_tiles)
                 copies[stratum - 1, j].wait_recv()
             block = held[stratum, span, :]
             half = block.astype(jnp.bfloat16)

time: 59.3 us -> 59.3 us (level)
  no operation moved by 1% of the time
where the time goes in v4:
time: 59.3 us; the launch traced here: 58.7 us
  Pallas kernels  57.1 us (96%)
  local copies, waits for them, and re-layouts  1.03 us (2%)
  between operations  0.64 us (1%)
    pallas_call x1, Pallas kernels, per_device(): pl.pallas_call(functools.partial(kernel, sizes), out_shape=pltpu.VMEM((ro...  57.1 us

profile of v4, /device:TPU:6, one launch (start us, length us, event | category | flops | bytes accessed | tf_op | source)
XLA Modules:
  0.0 58.7 jit_solution(4403196630573004570)
XLA Ops:
  0.6 57.1 %strata.1 = f32[1024,256]{1,0:T(8,128)S(1)} custom-call(s32[5]{0:T(128)} %bitcast.3, s32[5,2,8]{2,1,0:T(2,128)} %bitcast.2, f32[512,256]{1,0:T(8,128)} %rows_in.1, f32[512,256]{1,0:T(8,128)} %cols_in.1, bf16[5,8,128,128]{3,2,1,0:T(8,128)(2,1)} %tiles_in.1), custom_call_target="tpu_custom_call" | custom-call | tf_op jit(solution)/shard_map/strata/pallas_call | solution.py:171
  57.7 1.0 %fusion = (f32[512,256]{1,0:T(8,128)}, f32[512,256]{1,0:T(8,128)}) fusion(f32[1024,256]{1,0:T(8,128)S(1)} %strata.1), kind=kLoop, calls=%fused_computation | loop fusion | bytes 2097152 | tf_op jit(solution)/shard_map/slice | solution.py:202
